TPU v7x, 512 devices: a whole 4x8x8 slice. The times are simulated.
512 devices in a mesh: seq: 32 (over y, x), head: 16 (over z, core).
Axes of the slice: x: 4, y: 8, z: 8, core: 2. Of those that a mesh axis runs over, the one named last changes fastest.
Arguments:
- queries: float32 [32, 8192, 128], P('head', 'seq'), may hold values from -8 to 8
- keys: float32 [32, 8192, 128], P('head', 'seq'), may hold values from -8 to 8
- values: float32 [32, 8192, 128], P('head', 'seq'), may hold values from -6 to 6
- output: float32 [32, 8192, 128], P('head', 'seq'), may hold values from -3 to 3
- grad_output: float32 [32, 8192, 128], P(None, ('seq', 'head')), may hold values from -6 to 6
- mid_offsets: int32 [32, 9], P('head'), may hold values from 0 to 3
- far_offsets: int32 [32], P('head'), may hold values from 0 to 31
- drop_local: int32 [32, 8192, 64], P('head', 'seq'), may hold values from 0 to 4095
- drop_mid: int32 [32, 2048, 64], P('head', 'seq'), may hold values from 0 to 4095
- drop_far: int32 [32, 256, 64], P('head'), may hold values from 0 to 4095
Outputs:
- grad_queries: float32 [32, 8192, 128], P(None, ('seq', 'head'))
- grad_keys: float32 [32, 8192, 128], P(None, ('seq', 'head'))
- grad_values: float32 [32, 8192, 128], P(None, ('seq', 'head'))
All inputs are finite; a program needn't handle non-finite values.
Results may differ from a plain program's by a relative error of at most 0.0003.
Values sent between devices are 32-bit elements; how exact they have to be, the bound alone decides.
No kernel may reach another device: no remote copies, remote signals or barrier semaphores. Data moves between devices by JAX's collectives and lax.ppermute only.
A program may use at most 64 MiB of HBM per device.

v0:
```python
import jax
import jax.numpy as jnp
from jax import lax
from jax.sharding import PartitionSpec as P

GROUP = 4
keep_level = 7
keep_scale = 8.0 / 7.0
highest = lax.Precision.HIGHEST


def shifted(value, axis, steps):
    count = lax.axis_size(axis)
    initial, last = (max(0, -steps), min(count, count - steps))
    return lax.ppermute(value, axis, [(source, source + steps) for source in range(initial, last)])


def unpack_keep(words):
    bit_starts = jnp.arange(4, dtype=jnp.int32) * 3
    levels = jnp.bitwise_and(jnp.right_shift(words[..., None], bit_starts), 7)
    kept = jnp.where(levels < keep_level, keep_scale, 0.0).astype(jnp.float32)
    return kept.reshape(words.shape[:-1] + (words.shape[-1] * 4,))


def masked_lse(scores, allowed):
    return jax.nn.logsumexp(jnp.where(allowed, scores, -jnp.inf), axis=-1)


def chosen_mask(offsets, stride, extra_dims):
    chosen = jnp.arange(stride, dtype=jnp.int32)[None, None, :] == offsets[:, None, None]
    return chosen.reshape(chosen.shape + (1,) * extra_dims)


def pick_rows(source, offsets, stride):
    split_rows = source.reshape(
        (source.shape[0], source.shape[1] // stride, stride) + source.shape[2:]
    )
    chosen = chosen_mask(offsets, stride, source.ndim - 2)
    return jnp.sum(jnp.where(chosen, split_rows, 0.0), axis=2)


def add_rows(target, addend, offsets, stride):
    split_rows = target.reshape(
        (target.shape[0], target.shape[1] // stride, stride) + target.shape[2:]
    )
    chosen = chosen_mask(offsets, stride, target.ndim - 2)
    return (split_rows + jnp.where(chosen, jnp.expand_dims(addend, 2), 0.0)).reshape(target.shape)


def merge_lse(target, addend, offsets, stride):
    split_rows = target.reshape((target.shape[0], target.shape[1] // stride, stride))
    chosen = chosen_mask(offsets, stride, 0)
    merged = jnp.where(chosen, jnp.logaddexp(split_rows, jnp.expand_dims(addend, 2)), split_rows)
    return merged.reshape(target.shape)


def score_terms(scores, allowed, lse_rows, delta_rows, kept, value_rows, grad_rows):
    probs = jnp.where(allowed, jnp.exp(scores - lse_rows[..., None]), 0.0)
    dropped = probs * kept
    grad_probs = jnp.einsum("hqd,hkd->hqk", grad_rows, value_rows, precision=highest) * kept
    return (dropped, probs * (grad_probs - delta_rows[..., None]))


def per_device(
    queries,
    keys,
    values,
    output,
    grad_output,
    mid_offsets,
    far_offsets,
    drop_local,
    drop_mid,
    drop_far,
):
    row_count = queries.shape[1]
    score_scale = queries.shape[2] ** (-0.5)
    cycle_size = lax.axis_size("seq")
    cycle_place = lax.axis_index("seq")
    grad_rows = lax.all_to_all(grad_output, "head", split_axis=0, concat_axis=1, tiled=True)
    delta = jnp.sum(grad_rows * output, axis=-1)
    row_order = jnp.arange(row_count, dtype=jnp.int32)
    local_scores = jnp.einsum("hqd,hkd->hqk", queries, keys, precision=highest) * score_scale
    local_allowed = (row_order[:, None] >= row_order[None, :])[None]
    total_lse = masked_lse(local_scores, local_allowed)
    quarter_rows = row_count // GROUP
    shifted_place = cycle_place + GROUP // 2
    group_pos = shifted_place % GROUP
    mid_off = lax.dynamic_index_in_dim(mid_offsets, shifted_place // GROUP, 1, keepdims=False)
    mid_q = pick_rows(queries, mid_off, GROUP)
    mid_k = pick_rows(keys, mid_off, GROUP)
    mid_v = pick_rows(values, mid_off, GROUP)
    mid_grad = pick_rows(grad_rows, mid_off, GROUP)
    mid_delta = pick_rows(delta, mid_off, GROUP)
    mid_pair = jnp.stack([mid_k, mid_v])
    quarter_order = jnp.arange(quarter_rows, dtype=jnp.int32)
    key_blocks = [mid_k]
    value_blocks = [mid_v]
    allowed_blocks = [quarter_order[:, None] >= quarter_order[None, :]]
    mid_words = unpack_keep(drop_mid)
    keep_blocks = [lax.dynamic_slice_in_dim(mid_words, group_pos * quarter_rows, quarter_rows, 2)]
    for distance in range(1, GROUP):
        received = shifted(mid_pair, "seq", distance)
        key_blocks.append(received[0])
        value_blocks.append(received[1])
        allowed_blocks.append(
            jnp.broadcast_to(
                (group_pos >= distance) & (cycle_place >= distance), (quarter_rows, quarter_rows)
            )
        )
        keep_blocks.append(
            lax.dynamic_slice_in_dim(
                mid_words, jnp.maximum(group_pos - distance, 0) * quarter_rows, quarter_rows, 2
            )
        )
    mid_keys_all = jnp.concatenate(key_blocks, axis=1)
    mid_values_all = jnp.concatenate(value_blocks, axis=1)
    mid_allowed = jnp.concatenate(allowed_blocks, axis=1)[None]
    mid_keep = jnp.concatenate(keep_blocks, axis=2)
    mid_scores = jnp.einsum("hqd,hkd->hqk", mid_q, mid_keys_all, precision=highest) * score_scale
    mid_lse = masked_lse(mid_scores, mid_allowed)
    far_rows = row_count // cycle_size
    far_q = pick_rows(queries, far_offsets, cycle_size)
    far_k = pick_rows(keys, far_offsets, cycle_size)
    far_v = pick_rows(values, far_offsets, cycle_size)
    far_grad = pick_rows(grad_rows, far_offsets, cycle_size)
    far_delta = pick_rows(delta, far_offsets, cycle_size)
    far_all = lax.all_gather(jnp.stack([far_k, far_v]), "seq", axis=2, tiled=True)
    own_index = cycle_place * far_rows + jnp.arange(far_rows, dtype=jnp.int32)
    far_allowed = (row_order[None, :] <= own_index[:, None])[None]
    far_keep = unpack_keep(lax.dynamic_slice_in_dim(drop_far, cycle_place * far_rows, far_rows, 1))
    far_scores = jnp.einsum("hqd,hkd->hqk", far_q, far_all[0], precision=highest) * score_scale
    far_lse = masked_lse(far_scores, far_allowed)
    total_lse = merge_lse(total_lse, mid_lse, mid_off, GROUP)
    total_lse = merge_lse(total_lse, far_lse, far_offsets, cycle_size)
    local_keep = unpack_keep(drop_local)
    dropped, grad_scores = score_terms(
        local_scores, local_allowed, total_lse, delta, local_keep, values, grad_rows
    )
    grad_v = jnp.einsum("hqk,hqd->hkd", dropped, grad_rows, precision=highest)
    grad_q = jnp.einsum("hqk,hkd->hqd", grad_scores, keys, precision=highest) * score_scale
    grad_k = jnp.einsum("hqk,hqd->hkd", grad_scores, queries, precision=highest) * score_scale
    mid_lse_rows = pick_rows(total_lse, mid_off, GROUP)
    dropped, grad_scores = score_terms(
        mid_scores, mid_allowed, mid_lse_rows, mid_delta, mid_keep, mid_values_all, mid_grad
    )
    mid_gv = jnp.einsum("hqk,hqd->hkd", dropped, mid_grad, precision=highest)
    mid_gq = jnp.einsum("hqk,hkd->hqd", grad_scores, mid_keys_all, precision=highest) * score_scale
    mid_gk = jnp.einsum("hqk,hqd->hkd", grad_scores, mid_q, precision=highest) * score_scale
    own_gk = mid_gk[:, :quarter_rows]
    own_gv = mid_gv[:, :quarter_rows]
    for distance in range(1, GROUP):
        outgoing = jnp.stack(
            [
                mid_gk[:, distance * quarter_rows : (distance + 1) * quarter_rows],
                mid_gv[:, distance * quarter_rows : (distance + 1) * quarter_rows],
            ]
        )
        returned = shifted(outgoing, "seq", -distance)
        own_gk = own_gk + returned[0]
        own_gv = own_gv + returned[1]
    far_lse_rows = pick_rows(total_lse, far_offsets, cycle_size)
    dropped, grad_scores = score_terms(
        far_scores, far_allowed, far_lse_rows, far_delta, far_keep, far_all[1], far_grad
    )
    far_gq = jnp.einsum("hqk,hkd->hqd", grad_scores, far_all[0], precision=highest) * score_scale
    far_gv_all = jnp.einsum("hqk,hqd->hkd", dropped, far_grad, precision=highest)
    far_gk_all = jnp.einsum("hqk,hqd->hkd", grad_scores, far_q, precision=highest) * score_scale
    shares = lax.psum_scatter(
        jnp.stack([far_gk_all, far_gv_all]), "seq", scatter_dimension=2, tiled=True
    )
    far_gk = shares[0]
    far_gv = shares[1]
    grad_q = add_rows(add_rows(grad_q, mid_gq, mid_off, GROUP), far_gq, far_offsets, cycle_size)
    grad_k = add_rows(add_rows(grad_k, own_gk, mid_off, GROUP), far_gk, far_offsets, cycle_size)
    grad_v = add_rows(add_rows(grad_v, own_gv, mid_off, GROUP), far_gv, far_offsets, cycle_size)
    result = lax.all_to_all(
        jnp.stack([grad_q, grad_k, grad_v]), "head", split_axis=2, concat_axis=1, tiled=True
    )
    return (result[0], result[1], result[2])


def solution(mesh):
    placed = (
        P("head", "seq", None),
        P("head", "seq", None),
        P("head", "seq", None),
        P("head", "seq", None),
        P(None, ("seq", "head"), None),
        P("head", None),
        P("head"),
        P("head", "seq", None),
        P("head", "seq", None),
        P("head", None, None),
    )
    return jax.shard_map(
        per_device,
        mesh=mesh,
        in_specs=placed,
        out_specs=(
            P(None, ("seq", "head"), None),
            P(None, ("seq", "head"), None),
            P(None, ("seq", "head"), None),
        ),
        check_vma=False,
    )
```

profile of v0, /device:TPU:1, one launch (start us, length us, event | category | flops | bytes accessed | tf_op | source)
XLA Modules:
  0.0 363.3 jit_solution(801214255351252391)
XLA Ops:
  7.2 12.0 %all-to-all-start = ((f32[32,16,128]{2,1,0:T(8,128)}), f32[32,16,128]{2,1,0:T(8,128)S(1)}, u32[]{:S(2)}, u32[]{:S(2)}) async-start(f32[32,16,128]{2,1,0:T(8,128)} %param.14), calls=%async_computation | async-start | bytes 524288 | tf_op jit(solution)/shard_map/all_to_all | solution.py:80
  21.9 33.7 %all_gather.3 = f32[2,2,256,128]{3,2,1,0:T(8,128)S(1)} all-gather(f32[2,2,8,128]{3,2,1,0:T(8,128)S(1)} %pad_maximum_fusion.10), channel_id=1, replica_groups=mesh['seq'=32,'head'=16] {'seq'}, dimensions={2}, use_global_device_ids=true | all-gather | bytes 540672 | tf_op jit(solution)/shard_map/all_gather | solution.py:128
  58.3 0.8 constant_dynamic-slice_fusion.4
  61.2 0.7 reduce_max.32
  65.9 0.9 copy-done.6
  67.7 0.8 select_reduce_fusion.1
  68.5 4.0 %collective-permute-start.2 = (f32[2,2,64,128]{3,2,1,0:T(8,128)S(1)}, f32[2,2,64,128]{3,2,1,0:T(8,128)}, u32[]{:S(2)}, u32[]{:S(2)}) collective-permute-start(f32[2,2,64,128]{3,2,1,0:T(8,128)S(1)} %pad_maximum_fusion.5), channel_id=1, source_target_pairs={{0,48},{16,64},{32,80},{48,96},{64,112},{80,128},{96,144},{112,160... | collective-permute-start | bytes 393224 | tf_op jit(solution)/shard_map/ppermute | solution.py:15
  72.5 2.5 collective-permute-start.1
  75.0 1.8 collective-permute-start
  78.3 1.5 slice_bitcast_fusion.17
  84.1 0.8 select_reduce_fusion.11
  90.3 0.8 pad_maximum_fusion.1
  91.2 1.3 collective-permute-start.4
  92.5 1.3 collective-permute-start.5
  93.8 1.6 collective-permute-start.3
  97.5 1.3 collective-permute-done.4
  98.8 2.1 collective-permute-done.5
  101.1 212.0 %reduce-scatter.2.cloned.1.call-done = f32[2,2,8,128]{3,2,1,0:T(8,128)} async-done(((f32[2,2,256,128]{3,2,1,0:T(8,128)}), f32[2,2,8,128]{3,2,1,0:T(8,128)}) %reduce-scatter.2.cloned.1.call-update) | async-done | bytes 16400 | tf_op jit(solution)/shard_map/reduce_scatter | solution.py:169
  314.7 0.8 fusion.10
  315.5 1.0 fusion.5
  317.9 36.0 %all_to_all.33 = f32[3,2,256,128]{3,1,0,2:T(2,128)S(1)} all-to-all(f32[3,2,256,128]{3,1,0,2:T(2,128)S(1)} %copy.56), channel_id=1, replica_groups=mesh['seq'=32,'head'=16] {'head'}, dimensions={2} | all-to-all | bytes 1572864 | tf_op jit(solution)/shard_map/all_to_all | solution.py:177
  354.3 0.7 copy.59
  355.0 0.7 copy.58
  355.7 0.7 copy.57
  (198 shorter events, 28.7 us)
Async XLA Ops:
  7.2 51.9 %copy-start = (s32[2,256,64]{1,2,0:T(8,128)S(1)}, s32[2,256,64]{1,2,0:T(8,128)}, u32[]{:S(2)}) copy-start(s32[2,256,64]{1,2,0:T(8,128)} %param.19) | copy-start | bytes 393220
  7.2 58.7 %all-to-all-start = ((f32[32,16,128]{2,1,0:T(8,128)}), f32[32,16,128]{2,1,0:T(8,128)S(1)}, u32[]{:S(2)}, u32[]{:S(2)}) async-start(f32[32,16,128]{2,1,0:T(8,128)} %param.14), calls=%async_computation | async-start | bytes 524288 | tf_op jit(solution)/shard_map/all_to_all | solution.py:80
  19.2 294.0 %reduce-scatter.2.cloned.1.call-start = ((), (), s32[]{:S(2)}) async-start(), calls=%async_computation.3 | async-start | bytes 540672 | tf_op jit(solution)/shard_map/reduce_scatter | solution.py:169
  19.3 37.6 %copy-start.4 = (pred[256,256]{0,1:T(8,128)(4,1)}, pred[256,256]{0,1:T(8,128)(4,1)S(1)}, u32[]{:S(2)}) copy-start(pred[256,256]{0,1:T(8,128)(4,1)S(1)} %iota_compare_fusion) | copy-start | bytes 196612
  19.3 1.1 copy-start.17
  20.2 41.7 %copy-start.39 = (pred[2,4]{1,0:T(4,128)(4,1)}, pred[2,4]{1,0:T(4,128)(4,1)S(1)}, u32[]{:S(2)}) copy-start(pred[2,4]{1,0:T(4,128)(4,1)S(1)} %iota_compare_fusion.3) | copy-start | bytes 28
  20.3 38.9 %copy-start.42 = (pred[2,32]{1,0:T(4,128)(4,1)}, pred[2,32]{1,0:T(4,128)(4,1)S(1)}, u32[]{:S(2)}) copy-start(pred[2,32]{1,0:T(4,128)(4,1)S(1)} %iota_compare_fusion.4) | copy-start | bytes 196
  20.4 35.7 %copy-start.26 = (pred[8,256]{1,0:T(8,128)(4,1)}, pred[8,256]{1,0:T(8,128)(4,1)S(1)}, u32[]{:S(2)}) copy-start(pred[8,256]{1,0:T(8,128)(4,1)S(1)} %iota_compare_fusion.2) | copy-start | bytes 6148
  20.5 36.4 %copy-start.33 = (s32[256]{0:T(256)}, s32[256]{0:T(256)S(1)}, u32[]{:S(2)}) copy-start(s32[256]{0:T(256)S(1)} %shift_right_arithmetic.63) | copy-start | bytes 3076
  20.6 1.0 copy-start.2
  20.7 1.0 copy-start.1
  21.9 33.8 %copy-start.14 = (f32[2,8,128]{2,1,0:T(8,128)}, f32[2,8,128]{2,1,0:T(8,128)S(1)}, u32[]{:S(2)}) copy-start(f32[2,8,128]{2,1,0:T(8,128)S(1)} %get-tuple-element.12) | copy-start | bytes 24580
  56.9 4.4 %copy-start.28 = (f32[2,256]{1,0:T(2,128)}, f32[2,256]{1,0:T(2,128)S(1)}, u32[]{:S(2)}) copy-start(f32[2,256]{1,0:T(2,128)S(1)} %get-tuple-element.45) | copy-start | bytes 6148
  62.7 2.2 copy-start.13
  68.5 8.3 %copy-start.32 = (pred[2,16,16]{2,1,0:T(8,128)(4,1)S(1)}, pred[2,16,16]{2,1,0:T(8,128)(4,1)}, u32[]{:S(2)}) copy-start(pred[2,16,16]{2,1,0:T(8,128)(4,1)} %broadcast_in_dim.383) | copy-start | bytes 1540
  68.5 9.8 %collective-permute-start.2 = (f32[2,2,64,128]{3,2,1,0:T(8,128)S(1)}, f32[2,2,64,128]{3,2,1,0:T(8,128)}, u32[]{:S(2)}, u32[]{:S(2)}) collective-permute-start(f32[2,2,64,128]{3,2,1,0:T(8,128)S(1)} %pad_maximum_fusion.5), channel_id=1, source_target_pairs={{0,48},{16,64},{32,80},{48,96},{64,112},{80,128},{96,144},{112,160... | collective-permute-start | bytes 393224 | tf_op jit(solution)/shard_map/ppermute | solution.py:15
  72.5 7.3 %collective-permute-start.1 = (f32[2,2,64,128]{3,2,1,0:T(8,128)S(1)}, f32[2,2,64,128]{3,2,1,0:T(8,128)S(1)}, u32[]{:S(2)}, u32[]{:S(2)}) collective-permute-start(f32[2,2,64,128]{3,2,1,0:T(8,128)S(1)} %pad_maximum_fusion.5), channel_id=1, source_target_pairs={{0,32},{16,48},{32,64},{48,80},{64,96},{80,112},{96,128},{112,144}... | collective-permute-start | bytes 393224 | tf_op jit(solution)/shard_map/ppermute | solution.py:15
  75.0 5.5 %collective-permute-start = (f32[2,2,64,128]{3,2,1,0:T(8,128)S(1)}, f32[2,2,64,128]{3,2,1,0:T(8,128)S(1)}, u32[]{:S(2)}, u32[]{:S(2)}) collective-permute-start(f32[2,2,64,128]{3,2,1,0:T(8,128)S(1)} %pad_maximum_fusion.5), channel_id=1, source_target_pairs={{0,16},{16,32},{32,48},{48,64},{64,80},{80,96},{96,112},{112,128},... | collective-permute-start | bytes 393224 | tf_op jit(solution)/shard_map/ppermute | solution.py:15
  82.0 1.4 copy-start.7
  84.8 1.8 copy-start.44
  91.2 7.6 %collective-permute-start.4 = (f32[2,2,64,128]{3,2,1,0:T(8,128)S(1)}, f32[2,2,64,128]{3,2,1,0:T(8,128)S(1)}, u32[]{:S(2)}, u32[]{:S(2)}) collective-permute-start(f32[2,2,64,128]{3,2,1,0:T(8,128)S(1)} %pad_maximum_fusion.8), channel_id=1, source_target_pairs={{32,0},{48,16},{64,32},{80,48},{96,64},{112,80},{128,96},{144,112}... | collective-permute-start | bytes 393224 | tf_op jit(solution)/shard_map/ppermute | solution.py:15
  92.5 8.4 %collective-permute-start.5 = (f32[2,2,64,128]{3,2,1,0:T(8,128)S(1)}, f32[2,2,64,128]{3,2,1,0:T(8,128)S(1)}, u32[]{:S(2)}, u32[]{:S(2)}) collective-permute-start(f32[2,2,64,128]{3,2,1,0:T(8,128)S(1)} %pad_maximum_fusion.9), channel_id=1, source_target_pairs={{48,0},{64,16},{80,32},{96,48},{112,64},{128,80},{144,96},{160,112... | collective-permute-start | bytes 393224 | tf_op jit(solution)/shard_map/ppermute | solution.py:15
  93.8 1.9 copy-start.5
  93.8 7.2 %collective-permute-start.3 = (f32[2,2,64,128]{3,2,1,0:T(8,128)S(1)}, f32[2,2,64,128]{3,2,1,0:T(8,128)S(1)}, u32[]{:S(2)}, u32[]{:S(2)}) collective-permute-start(f32[2,2,64,128]{3,2,1,0:T(8,128)S(1)} %pad_maximum_fusion.7), channel_id=1, source_target_pairs={{16,0},{32,16},{48,32},{64,48},{80,64},{96,80},{112,96},{128,112},... | collective-permute-start | bytes 393224 | tf_op jit(solution)/shard_map/ppermute | solution.py:15
  (35 other events, 26.5 us)
Sparse Core Ops, SparseCore 0:
  91.3 221.8 reduce-scatter.1
where the time goes:
time: 364 us; the launch traced here: 363 us
  waiting for transfers between devices  216 us (59%)
  blocking collectives  69.7 us (19%)
  starting transfers between devices  24.5 us (7%)
  local copies, waits for them, and re-layouts  23.7 us (7%)
  between operations  14.9 us (4%)
  matrix products  8.36 us (2%)
  other arithmetic  6.66 us (2%)
    reduce_scatter x1, waiting for transfers between devices, per_device(): lax.psum_scatter(jnp.stack([far_gk_all, far_gv_all]), 'seq', scatter_dime...  212 us
    all_to_all x1, blocking collectives, per_device(): lax.all_to_all(jnp.stack([grad_q, grad_k, grad_v]), 'head', split_axis=2,...  36 us
    all_gather x1, blocking collectives, per_device(): lax.all_gather(jnp.stack([far_k, far_v]), 'seq', axis=2, tiled=True)  33.7 us
    ppermute x6, starting transfers between devices, shifted(): lax.ppermute(value, axis, [(source, source + steps) for source in range(i...  12.5 us
    all_to_all x1, starting transfers between devices, per_device(): lax.all_to_all(grad_output, 'head', split_axis=0, concat_axis=1, tiled=True)  12 us
    unnamed x103, local copies, waits for them, and re-layouts  8.8 us
  transfers between devices with their start and end apart: 8, of which 4 were waited for; matrix products, arithmetic and copies ran while one was open for 4% of the time, Pallas kernels for 0%

commit v1 on v0

--- a/solution.py
+++ b/solution.py
@@ -125,7 +125,10 @@
     far_v = pick_rows(values, far_offsets, cycle_size)
     far_grad = pick_rows(grad_rows, far_offsets, cycle_size)
     far_delta = pick_rows(delta, far_offsets, cycle_size)
-    far_all = lax.all_gather(jnp.stack([far_k, far_v]), "seq", axis=2, tiled=True)
+    far_all = jnp.concatenate(
+        lax.all_to_all(jnp.stack([jnp.stack([far_k, far_v])] * lax.axis_size("seq")), "seq", 0, 0),
+        axis=2,
+    )
     own_index = cycle_place * far_rows + jnp.arange(far_rows, dtype=jnp.int32)
     far_allowed = (row_order[None, :] <= own_index[:, None])[None]
     far_keep = unpack_keep(lax.dynamic_slice_in_dim(drop_far, cycle_place * far_rows, far_rows, 1))

time: 364 us -> 339 us (0.931)
  blocking collectives: 69.7 us -> 36.2 us
  starting transfers between devices: 24.5 us -> 36 us
    all_gather x1 -> x0, blocking collectives: 33.7 us -> none  [per_device(): lax.all_gather(jnp.stack([far_k, far_v]), 'seq', axis=2, tiled=True)]
    all_to_all x0 -> x1, starting transfers between devices: none -> 9.67 us  [per_device(): lax.all_to_all(jnp.stack([jnp.stack([far_k, far_v])] * lax.axis_size('seq...]
    reduce_scatter x1, waiting for transfers between devices: 212 us -> 203 us  [per_device(): lax.psum_scatter(jnp.stack([far_gk_all, far_gv_all]), 'seq', scatter_dime...]
    unnamed x103 -> x81, local copies, waits for them, and re-layouts: 8.8 us -> 10.1 us
  transfers between devices with their start and end apart: 8 -> 9, of which waited for: 4 -> 5; matrix products, arithmetic and copies ran while one was open for 4% -> 4% of each run, Pallas kernels for 0% -> 0%
where the time goes in v1:
time: 339 us; the launch traced here: 338 us
  waiting for transfers between devices  213 us (63%)
  blocking collectives  36.2 us (11%)
  starting transfers between devices  36 us (11%)
  local copies, waits for them, and re-layouts  23.6 us (7%)
  between operations  14.7 us (4%)
  matrix products  8.37 us (2%)
  other arithmetic  6.06 us (2%)
    reduce_scatter x1, waiting for transfers between devices, per_device(): lax.psum_scatter(jnp.stack([far_gk_all, far_gv_all]), 'seq', scatter_dime...  203 us
    all_to_all x1, blocking collectives, per_device(): lax.all_to_all(jnp.stack([grad_q, grad_k, grad_v]), 'head', split_axis=2,...  36.2 us
    ppermute x6, starting transfers between devices, shifted(): lax.ppermute(value, axis, [(source, source + steps) for source in range(i...  14.3 us
    all_to_all x1, starting transfers between devices, per_device(): lax.all_to_all(grad_output, 'head', split_axis=0, concat_axis=1, tiled=True)  12 us
    unnamed x81, local copies, waits for them, and re-layouts  10.1 us
    all_to_all x1, starting transfers between devices, per_device(): lax.all_to_all(jnp.stack([jnp.stack([far_k, far_v])] * lax.axis_size('seq...  9.67 us
  transfers between devices with their start and end apart: 9, of which 5 were waited for; matrix products, arithmetic and copies ran while one was open for 4% of the time, Pallas kernels for 0%

profile of v1, /device:TPU:1, one launch (start us, length us, event | category | flops | bytes accessed | tf_op | source)
XLA Modules:
  0.0 337.8 jit_solution(2791056139395050232)
XLA Ops:
  7.2 12.0 %all-to-all-start.1 = ((f32[32,16,128]{2,1,0:T(8,128)}), f32[32,16,128]{2,1,0:T(8,128)S(1)}, u32[]{:S(2)}, u32[]{:S(2)}) async-start(f32[32,16,128]{2,1,0:T(8,128)} %param.14), calls=%async_computation.1 | async-start | bytes 524288 | tf_op jit(solution)/shard_map/all_to_all | solution.py:80
  23.5 0.8 constant_dynamic-slice_fusion.4
  26.2 0.8 copy-done.9
  27.5 3.3 all-to-all-done.1
  30.9 0.8 stack.46
  31.7 9.7 %all-to-all-start = ((f32[32,2,2,8,128]{4,3,2,1,0:T(8,128)}), f32[32,2,2,8,128]{4,3,2,1,0:T(8,128)S(1)}, u32[]{:S(2)}, u32[]{:S(2)}) async-start(f32[32,2,2,8,128]{4,3,2,1,0:T(8,128)} %stack.46), calls=%async_computation | async-start | bytes 1048576 | tf_op jit(solution)/shard_map/all_to_all | solution.py:129
  41.5 0.9 copy-done.4
  43.3 0.8 select_reduce_fusion.1
  44.1 5.0 %collective-permute-start.2 = (f32[2,2,64,128]{3,2,1,0:T(8,128)S(1)}, f32[2,2,64,128]{3,2,1,0:T(8,128)}, u32[]{:S(2)}, u32[]{:S(2)}) collective-permute-start(f32[2,2,64,128]{3,2,1,0:T(8,128)S(1)} %pad_maximum_fusion.5), channel_id=1, source_target_pairs={{0,48},{16,64},{32,80},{48,96},{64,112},{80,128},{96,144},{112,160... | collective-permute-start | bytes 393224 | tf_op jit(solution)/shard_map/ppermute | solution.py:15
  49.1 3.4 collective-permute-start.1
  52.5 1.9 collective-permute-start
  55.9 1.5 slice_bitcast_fusion.12
  58.1 0.9 collective-permute-done
  64.6 0.8 select_reduce_fusion.11
  70.9 0.8 pad_maximum_fusion.1
  71.8 1.3 collective-permute-start.4
  73.1 1.3 collective-permute-start.5
  74.4 1.5 collective-permute-start.3
  78.1 3.2 collective-permute-done.4
  81.2 2.7 collective-permute-done.5
  84.0 202.7 %reduce-scatter.2.cloned.1.call-done = f32[2,2,8,128]{3,2,1,0:T(8,128)} async-done(((f32[2,2,256,128]{3,2,1,0:T(8,128)}), f32[2,2,8,128]{3,2,1,0:T(8,128)}) %reduce-scatter.2.cloned.1.call-update) | async-done | bytes 16400 | tf_op jit(solution)/shard_map/reduce_scatter | solution.py:172
  288.9 0.8 fusion.10
  289.8 1.0 fusion.5
  292.1 36.2 %all_to_all.38 = f32[3,2,256,128]{3,1,0,2:T(2,128)S(1)} all-to-all(f32[3,2,256,128]{3,1,0,2:T(2,128)S(1)} %copy.62), channel_id=1, replica_groups=mesh['seq'=32,'head'=16] {'head'}, dimensions={2} | all-to-all | bytes 1572864 | tf_op jit(solution)/shard_map/all_to_all | solution.py:180
  (179 shorter events, 29.1 us)
Async XLA Ops:
  7.2 15.5 %copy-start = (s32[2,256,64]{1,2,0:T(8,128)S(1)}, s32[2,256,64]{1,2,0:T(8,128)}, u32[]{:S(2)}) copy-start(s32[2,256,64]{1,2,0:T(8,128)} %param.19) | copy-start | bytes 393220
  7.2 23.7 %all-to-all-start.1 = ((f32[32,16,128]{2,1,0:T(8,128)}), f32[32,16,128]{2,1,0:T(8,128)S(1)}, u32[]{:S(2)}, u32[]{:S(2)}) async-start(f32[32,16,128]{2,1,0:T(8,128)} %param.14), calls=%async_computation.1 | async-start | bytes 524288 | tf_op jit(solution)/shard_map/all_to_all | solution.py:80
  19.2 1.2 copy-start.12
  20.1 23.2 %copy-start.32 = (pred[2,4]{1,0:T(4,128)(4,1)}, pred[2,4]{1,0:T(4,128)(4,1)S(1)}, u32[]{:S(2)}) copy-start(pred[2,4]{1,0:T(4,128)(4,1)S(1)} %iota_compare_fusion.3) | copy-start | bytes 28
  20.2 4.2 %copy-start.34 = (pred[2,32]{1,0:T(4,128)(4,1)}, pred[2,32]{1,0:T(4,128)(4,1)S(1)}, u32[]{:S(2)}) copy-start(pred[2,32]{1,0:T(4,128)(4,1)S(1)} %iota_compare_fusion.4) | copy-start | bytes 196
  20.5 1.0 copy-start.2
  20.6 1.0 copy-start.1
  21.5 0.9 copy-start.3
  31.7 30.0 %all-to-all-start = ((f32[32,2,2,8,128]{4,3,2,1,0:T(8,128)}), f32[32,2,2,8,128]{4,3,2,1,0:T(8,128)S(1)}, u32[]{:S(2)}, u32[]{:S(2)}) async-start(f32[32,2,2,8,128]{4,3,2,1,0:T(8,128)} %stack.46), calls=%async_computation | async-start | bytes 1048576 | tf_op jit(solution)/shard_map/all_to_all | solution.py:129
  41.4 245.3 %reduce-scatter.2.cloned.1.call-start = ((), (), s32[]{:S(2)}) async-start(), calls=%async_computation.4 | async-start | bytes 540672 | tf_op jit(solution)/shard_map/reduce_scatter | solution.py:172
  41.4 1.0 copy-start.4
  44.1 11.8 %collective-permute-start.2 = (f32[2,2,64,128]{3,2,1,0:T(8,128)S(1)}, f32[2,2,64,128]{3,2,1,0:T(8,128)}, u32[]{:S(2)}, u32[]{:S(2)}) collective-permute-start(f32[2,2,64,128]{3,2,1,0:T(8,128)S(1)} %pad_maximum_fusion.5), channel_id=1, source_target_pairs={{0,48},{16,64},{32,80},{48,96},{64,112},{80,128},{96,144},{112,160... | collective-permute-start | bytes 393224 | tf_op jit(solution)/shard_map/ppermute | solution.py:15
  49.1 8.3 %collective-permute-start.1 = (f32[2,2,64,128]{3,2,1,0:T(8,128)S(1)}, f32[2,2,64,128]{3,2,1,0:T(8,128)S(1)}, u32[]{:S(2)}, u32[]{:S(2)}) collective-permute-start(f32[2,2,64,128]{3,2,1,0:T(8,128)S(1)} %pad_maximum_fusion.5), channel_id=1, source_target_pairs={{0,32},{16,48},{32,64},{48,80},{64,96},{80,112},{96,128},{112,144}... | collective-permute-start | bytes 393224 | tf_op jit(solution)/shard_map/ppermute | solution.py:15
  52.5 6.5 %collective-permute-start = (f32[2,2,64,128]{3,2,1,0:T(8,128)S(1)}, f32[2,2,64,128]{3,2,1,0:T(8,128)S(1)}, u32[]{:S(2)}, u32[]{:S(2)}) collective-permute-start(f32[2,2,64,128]{3,2,1,0:T(8,128)S(1)} %pad_maximum_fusion.5), channel_id=1, source_target_pairs={{0,16},{16,32},{32,48},{48,64},{64,80},{80,96},{96,112},{112,128},... | collective-permute-start | bytes 393224 | tf_op jit(solution)/shard_map/ppermute | solution.py:15
  57.4 2.2 copy-start.13
  58.1 1.6 copy-start.15
  63.9 1.6 copy-start.8
  64.6 0.9 copy-start.5
  64.6 0.9 copy-start.6
  64.6 0.9 copy-start.7
  71.8 9.4 %collective-permute-start.4 = (f32[2,2,64,128]{3,2,1,0:T(8,128)S(1)}, f32[2,2,64,128]{3,2,1,0:T(8,128)S(1)}, u32[]{:S(2)}, u32[]{:S(2)}) collective-permute-start(f32[2,2,64,128]{3,2,1,0:T(8,128)S(1)} %pad_maximum_fusion.8), channel_id=1, source_target_pairs={{32,0},{48,16},{64,32},{80,48},{96,64},{112,80},{128,96},{144,112}... | collective-permute-start | bytes 393224 | tf_op jit(solution)/shard_map/ppermute | solution.py:15
  73.1 10.8 %collective-permute-start.5 = (f32[2,2,64,128]{3,2,1,0:T(8,128)S(1)}, f32[2,2,64,128]{3,2,1,0:T(8,128)S(1)}, u32[]{:S(2)}, u32[]{:S(2)}) collective-permute-start(f32[2,2,64,128]{3,2,1,0:T(8,128)S(1)} %pad_maximum_fusion.9), channel_id=1, source_target_pairs={{48,0},{64,16},{80,32},{96,48},{112,64},{128,80},{144,96},{160,112... | collective-permute-start | bytes 393224 | tf_op jit(solution)/shard_map/ppermute | solution.py:15
  74.4 9.5 %collective-permute-start.3 = (f32[2,2,64,128]{3,2,1,0:T(8,128)S(1)}, f32[2,2,64,128]{3,2,1,0:T(8,128)S(1)}, u32[]{:S(2)}, u32[]{:S(2)}) collective-permute-start(f32[2,2,64,128]{3,2,1,0:T(8,128)S(1)} %pad_maximum_fusion.7), channel_id=1, source_target_pairs={{16,0},{32,16},{48,32},{64,48},{80,64},{96,80},{112,96},{128,112},... | collective-permute-start | bytes 393224 | tf_op jit(solution)/shard_map/ppermute | solution.py:15
  76.8 1.0 copy-start.18
  (25 other events, 18.7 us)
Sparse Core Ops, SparseCore 0:
  71.9 214.7 reduce-scatter.1
